TPU v7x, 32 devices: a whole 2x2x4 slice. The times are simulated.
32 devices in a mesh: dp: 8 (over z, x), tensor: 4 (over y, core).
Axes of the slice: x: 2, y: 2, z: 4, core: 2. Of those that a mesh axis runs over, the one named last changes fastest.
Arguments:
- hidden_in: bfloat16 [32768, 768], P(('dp', 'tensor')), may hold values from -6 to 6
- teacher: float32 [32768, 768], P(('dp', 'tensor')), may hold values from -6 to 6
- valid_mask: int32 [32768], P(('dp', 'tensor')), may hold values from 0 to 1
- random_blocks: int32 [12, 32, 3, 32], replicated, may hold values from 0 to 1, as said below
- w_qkv: bfloat16 [3, 768, 768], P(None, 'dp', 'tensor'), may hold values from -0.21875 to 0.21875
- b_qv: bfloat16 [2, 12, 64], P(None, 'tensor', 'dp'), may hold values from -3 to 3
- w_out: bfloat16 [768, 768], P('tensor', 'dp'), may hold values from -3 to 3
- w_in: bfloat16 [768, 3072], P('dp', 'tensor'), may hold values from -0.21875 to 0.21875
- b_in: bfloat16 [48, 64], P('tensor', 'dp'), may hold values from -3 to 3
- w_back: bfloat16 [3072, 768], P('tensor', 'dp'), may hold values from -0.109375 to 0.109375
- ln_gains: bfloat16 [2, 768], P(None, 'dp'), may hold values from 0.25 to 1.75
- row_biases: bfloat16 [4, 768], P(None, 'dp'), may hold values from -2 to 2
Outputs:
- loss: float32 [], replicated
- encoded: float32 [32768, 768], P(('dp', 'tensor'))
- grad_in: float32 [32768, 768], P(('dp', 'tensor'))
- grad_qkv: float32 [3, 768, 768], P(None, 'dp', 'tensor')
- grad_qv_bias: float32 [2, 12, 64], P(None, 'tensor', 'dp')
- grad_out: float32 [768, 768], P('tensor', 'dp')
- grad_w_in: float32 [768, 3072], P('dp', 'tensor')
- grad_b_in: float32 [48, 64], P('tensor', 'dp')
- grad_w_back: float32 [3072, 768], P('tensor', 'dp')
- grad_gains: float32 [2, 768], P(None, ('dp', 'tensor'))
- grad_biases: float32 [4, 768], P(None, ('dp', 'tensor'))
Inputs may be any that keep to these rules, and one draw needn't show every extreme that they name: `random_blocks`: each [h, j, r, :] holds a single 1; the 3 blocks chosen for one h and j are different, and none of them is block 0, block 31, or within one block of j.
All inputs are finite; a program needn't handle non-finite values.
Results may differ from a plain program's by a relative error of at most 0.015.
Values may be sent and summed in bfloat16 or wider, within the bound.
A program may use at most 192 MiB of HBM per device.

v0:
```python
import jax
import jax.numpy as jnp
from jax import lax
from jax.sharding import PartitionSpec as P

D = 768
HD = 64
BLK = 64
SEQ_LEN = 2048
epsilon = 1e-06
masked_score = -1e30
exact_precision = lax.Precision.HIGHEST


def layer_norm(values, gain, shift):
    centred = values - jnp.mean(values, axis=-1, keepdims=True)
    variance = jnp.mean(centred * centred, axis=-1, keepdims=True)
    return centred * lax.rsqrt(variance + epsilon) * gain + shift


def gelu_tanh(values):
    return (
        0.5
        * values
        * (1.0 + jnp.tanh(0.7978845608028654 * (values + 0.044715 * values * values * values)))
    )


def fetch_weights(w_qkv, b_qv, w_out, w_in, b_in, w_back, ln_gains, row_biases):
    return (
        lax.all_gather(w_qkv, "dp", axis=1, tiled=True),
        lax.all_gather(b_qv, "dp", axis=2, tiled=True),
        lax.all_gather(w_out, "dp", axis=1, tiled=True),
        lax.all_gather(w_in, "dp", axis=0, tiled=True),
        lax.all_gather(b_in, "dp", axis=1, tiled=True),
        lax.all_gather(w_back, "dp", axis=1, tiled=True),
        lax.all_gather(ln_gains, "dp", axis=1, tiled=True),
        lax.all_gather(row_biases, "dp", axis=1, tiled=True),
    )


def widen_units(in_weight, in_bias, back_weight):
    return (
        lax.all_gather(in_weight, "tensor", axis=1, tiled=True),
        lax.all_gather(in_bias, "tensor", axis=0, tiled=True),
        lax.all_gather(back_weight, "tensor", axis=0, tiled=True),
    )


def gather_slots(blocks, one_hot):
    middle = one_hot.shape[0]
    nearby = jnp.stack([blocks[0:middle], blocks[1 : middle + 1], blocks[2 : middle + 2]], axis=1)
    edges = jnp.broadcast_to(
        jnp.stack([blocks[0], blocks[-1]])[None], (middle, 2) + blocks.shape[1:]
    )
    distant = jnp.einsum(
        "mrn,nbd->mrbd", one_hot, blocks, preferred_element_type=jnp.float32
    ).astype(jnp.bfloat16)
    slots = jnp.concatenate([nearby, edges, distant], axis=1)
    return slots.reshape(middle, -1, blocks.shape[-1])


def slot_valid(middle, width):
    slot_ids = jnp.arange(width) // BLK
    row_ids = jnp.arange(middle)[:, None]
    first_double = (slot_ids[None, :] == 3) & (row_ids == 0)
    last_double = (slot_ids[None, :] == 4) & (row_ids == middle - 1)
    return jnp.logical_not(first_double | last_double)[:, None, :]


def spread_slots(slot_grads, one_hot):
    middle = slot_grads.shape[0]
    parts_grad = slot_grads.reshape(middle, -1, BLK, slot_grads.shape[-1])
    nearby = (
        jnp.pad(parts_grad[:, 0], ((0, 2), (0, 0), (0, 0)))
        + jnp.pad(parts_grad[:, 1], ((1, 1), (0, 0), (0, 0)))
        + jnp.pad(parts_grad[:, 2], ((2, 0), (0, 0), (0, 0)))
    )
    edges = jnp.concatenate(
        [
            jnp.sum(parts_grad[:, 3], axis=0)[None],
            jnp.zeros((middle,) + parts_grad.shape[2:], jnp.float32),
            jnp.sum(parts_grad[:, 4], axis=0)[None],
        ],
        axis=0,
    )
    distant = jnp.einsum(
        "mrn,mrbd->nbd", one_hot.astype(jnp.float32), parts_grad[:, 5:], precision=exact_precision
    )
    return nearby + edges + distant


def log_total(scores):
    peak = jnp.max(scores, axis=-1, keepdims=True)
    return peak + jnp.log(jnp.sum(jnp.exp(scores - peak), axis=-1, keepdims=True))


def middle_scores(stack, chosen):
    queries, keys, values = (stack[0], stack[1], stack[2])
    scale = queries.shape[-1] ** (-0.5)
    one_hot = chosen[1:-1].astype(jnp.bfloat16)
    mid_queries = queries[1:-1]
    key_slots = gather_slots(keys, one_hot)
    value_slots = gather_slots(values, one_hot)
    scores = (
        jnp.einsum("mqd,mkd->mqk", mid_queries, key_slots, preferred_element_type=jnp.float32)
        * scale
    )
    scores = jnp.where(slot_valid(mid_queries.shape[0], key_slots.shape[1]), scores, masked_score)
    return (mid_queries, key_slots, value_slots, scores)


def edge_scores_of(stack):
    queries, keys, values = (stack[0], stack[1], stack[2])
    head_dim = queries.shape[-1]
    edge_queries = jnp.concatenate([queries[0], queries[-1]], axis=0)
    flat_keys = keys.reshape(-1, head_dim)
    flat_values = values.reshape(-1, head_dim)
    scores = jnp.einsum(
        "qd,kd->qk", edge_queries, flat_keys, preferred_element_type=jnp.float32
    ) * head_dim ** (-0.5)
    return (edge_queries, flat_keys, flat_values, scores)


def item_forward(stack, chosen):
    mid_queries, key_slots, value_slots, scores = middle_scores(stack, chosen)
    log_middle = log_total(scores)
    shares = jnp.exp(scores - log_middle).astype(jnp.bfloat16)
    context_mid = jnp.einsum(
        "mqk,mkd->mqd", shares, value_slots, preferred_element_type=jnp.float32
    )
    edge_queries, flat_keys, flat_values, edge_scores = edge_scores_of(stack)
    log_edge = log_total(edge_scores)
    edge_shares = jnp.exp(edge_scores - log_edge).astype(jnp.bfloat16)
    context_edge = jnp.dot(edge_shares, flat_values, preferred_element_type=jnp.float32)
    block = stack.shape[2]
    context = jnp.concatenate(
        [context_edge[:block][None], context_mid, context_edge[block:][None]], axis=0
    )
    return (context.astype(jnp.bfloat16), log_middle[..., 0], log_edge[:, 0])


def item_backward(stack, chosen, grad_context, log_middle, log_edge):
    scale = stack.shape[-1] ** (-0.5)
    block = stack.shape[2]
    mid_queries, key_slots, value_slots, scores = middle_scores(stack, chosen)
    shares = jnp.exp(scores - log_middle[..., None])
    grad_mid = grad_context[1:-1]
    grad_shares = jnp.einsum(
        "mqd,mkd->mqk", grad_mid, value_slots, preferred_element_type=jnp.float32
    )
    inner = jnp.sum(shares * grad_shares, axis=-1, keepdims=True)
    grad_scores = (shares * (grad_shares - inner)).astype(jnp.bfloat16)
    grad_query_mid = (
        jnp.einsum("mqk,mkd->mqd", grad_scores, key_slots, preferred_element_type=jnp.float32)
        * scale
    )
    grad_key_slots = (
        jnp.einsum("mqk,mqd->mkd", grad_scores, mid_queries, preferred_element_type=jnp.float32)
        * scale
    )
    grad_value_slots = jnp.einsum(
        "mqk,mqd->mkd", shares.astype(jnp.bfloat16), grad_mid, preferred_element_type=jnp.float32
    )
    edge_queries, flat_keys, flat_values, edge_scores = edge_scores_of(stack)
    edge_shares = jnp.exp(edge_scores - log_edge[:, None])
    grad_edge = jnp.concatenate([grad_context[0], grad_context[-1]], axis=0)
    grad_edge_shares = jnp.einsum(
        "qd,kd->qk", grad_edge, flat_values, preferred_element_type=jnp.float32
    )
    edge_inner = jnp.sum(edge_shares * grad_edge_shares, axis=-1, keepdims=True)
    grad_edge_scores = (edge_shares * (grad_edge_shares - edge_inner)).astype(jnp.bfloat16)
    grad_query_edge = (
        jnp.dot(grad_edge_scores, flat_keys, preferred_element_type=jnp.float32) * scale
    )
    grad_key_edge = (
        jnp.einsum("qk,qd->kd", grad_edge_scores, edge_queries, preferred_element_type=jnp.float32)
        * scale
    )
    grad_value_edge = jnp.einsum(
        "qk,qd->kd", edge_shares.astype(jnp.bfloat16), grad_edge, preferred_element_type=jnp.float32
    )
    one_hot = chosen[1:-1]
    grad_queries = jnp.concatenate(
        [grad_query_edge[:block][None], grad_query_mid, grad_query_edge[block:][None]], axis=0
    )
    grad_keys = spread_slots(grad_key_slots, one_hot) + grad_key_edge.reshape(stack.shape[1:])
    grad_values = spread_slots(grad_value_slots, one_hot) + grad_value_edge.reshape(stack.shape[1:])
    return jnp.stack([grad_queries, grad_keys, grad_values]).astype(jnp.bfloat16)


def run_forward(pair):
    return item_forward(pair[0], pair[1])


def run_backward(group_items):
    return item_backward(
        group_items[0], group_items[1], group_items[2], group_items[3], group_items[4]
    )


def per_device(
    hidden_in,
    teacher,
    valid_mask,
    random_blocks,
    w_qkv,
    b_qv,
    w_out,
    w_in,
    b_in,
    w_back,
    ln_gains,
    row_biases,
):
    local_rows = hidden_in.shape[0]
    tensor_count = lax.axis_size("tensor")
    tokens_total = local_rows * tensor_count * lax.axis_size("dp")
    group_rows = local_rows * tensor_count
    seq_count = group_rows // SEQ_LEN
    blocks_count = SEQ_LEN // BLK
    fetched = fetch_weights(w_qkv, b_qv, w_out, w_in, b_in, w_back, ln_gains, row_biases)
    qkv_weight, bias_pair, out_weight, in_weight, in_bias, back_weight, gains, biases = fetched
    full_in, full_bias, full_back = widen_units(in_weight, in_bias, back_weight)
    head_local = qkv_weight.shape[2] // HD
    chosen_local = lax.dynamic_slice_in_dim(
        random_blocks, lax.axis_index("tensor") * head_local, head_local, 0
    )
    whole_in = lax.all_gather(hidden_in, "tensor", axis=0, tiled=True)
    projected = jnp.einsum("nd,kde->kne", whole_in, qkv_weight, preferred_element_type=jnp.float32)
    bias_flat = bias_pair.astype(jnp.float32).reshape(2, -1)
    bias_rows = jnp.stack([bias_flat[0], jnp.zeros_like(bias_flat[0]), bias_flat[1]])
    projected = (projected + bias_rows[:, None, :]).astype(jnp.bfloat16)
    items = projected.reshape(3, seq_count, blocks_count, BLK, head_local, HD).transpose(
        1, 4, 0, 2, 3, 5
    )
    items = items.reshape(seq_count * head_local, 3, blocks_count, BLK, HD)
    chosen_all = jnp.tile(chosen_local, (seq_count, 1, 1, 1))
    context_items, log_middle, log_edge = lax.map(run_forward, (items, chosen_all))
    context = context_items.reshape(seq_count, head_local, blocks_count, BLK, HD).transpose(
        0, 2, 3, 1, 4
    )
    context = context.reshape(group_rows, head_local * HD)
    piece = context
    attention = lax.psum_scatter(
        jnp.dot(piece, out_weight, preferred_element_type=jnp.float32).astype(jnp.bfloat16),
        "tensor",
        scatter_dimension=0,
        tiled=True,
    ).astype(jnp.float32)
    gain_values = gains.astype(jnp.float32)
    bias_values = biases.astype(jnp.float32)
    mixed = hidden_in.astype(jnp.float32) + attention + bias_values[0]
    normed, first_back = jax.vjp(layer_norm, mixed, gain_values[0], bias_values[1])
    normed_low = normed.astype(jnp.bfloat16)
    inner = jnp.dot(normed_low, full_in, preferred_element_type=jnp.float32) + full_bias.astype(
        jnp.float32
    ).reshape(-1)
    active_float, gelu_back = jax.vjp(gelu_tanh, inner)
    active = active_float.astype(jnp.bfloat16)
    feed = jnp.dot(active, full_back, preferred_element_type=jnp.float32)
    second = normed + feed + bias_values[2]
    encoded, final_back = jax.vjp(layer_norm, second, gain_values[1], bias_values[3])
    mask_rows = valid_mask.astype(jnp.float32)
    error = encoded - teacher
    sum_sq, valid_total = lax.psum(
        (jnp.sum(mask_rows[:, None] * error * error), jnp.sum(mask_rows)), ("dp", "tensor")
    )
    loss = sum_sq / (D * valid_total)
    grad_encoded = mask_rows[:, None] * error * (tokens_total / valid_total)
    grad_second, grad_gain_two, grad_shift_two = final_back(grad_encoded)
    second_low = grad_second.astype(jnp.bfloat16)
    fetched = fetch_weights(w_qkv, b_qv, w_out, w_in, b_in, w_back, ln_gains, row_biases)
    qkv_weight, bias_pair, out_weight, in_weight, in_bias, back_weight, gains, biases = fetched
    full_in, full_bias, full_back = widen_units(in_weight, in_bias, back_weight)
    grad_active = jnp.einsum("nd,fd->nf", second_low, full_back, preferred_element_type=jnp.float32)
    grad_inner = gelu_back(grad_active)[0].astype(jnp.bfloat16)
    grad_in_full = jnp.einsum(
        "nd,nf->df", normed_low, grad_inner, preferred_element_type=jnp.float32
    )
    grad_back_full = jnp.einsum("nf,nd->fd", active, second_low, preferred_element_type=jnp.float32)
    grad_bias_full = jnp.sum(grad_inner, axis=0, dtype=jnp.float32).reshape(-1, 64)
    grad_in_weight, grad_in_bias, grad_back_weight = (
        lax.psum_scatter(
            grad_in_full.astype(jnp.bfloat16), "tensor", scatter_dimension=1, tiled=True
        ).astype(jnp.float32),
        lax.psum_scatter(
            grad_bias_full.astype(jnp.bfloat16), "tensor", scatter_dimension=0, tiled=True
        ).astype(jnp.float32),
        lax.psum_scatter(
            grad_back_full.astype(jnp.bfloat16), "tensor", scatter_dimension=0, tiled=True
        ).astype(jnp.float32),
    )
    grad_feed = jnp.einsum("nf,df->nd", grad_inner, full_in, preferred_element_type=jnp.float32)
    grad_normed = grad_second + grad_feed
    grad_mixed, grad_gain_one, grad_shift_one = first_back(grad_normed)
    mixed_low = grad_mixed.astype(jnp.bfloat16)
    whole_grad_mixer = lax.all_gather(mixed_low, "tensor", axis=0, tiled=True)
    grad_context = jnp.einsum(
        "nd,ed->ne", whole_grad_mixer, out_weight, preferred_element_type=jnp.float32
    ).astype(jnp.bfloat16)
    grad_out_weight = jnp.einsum(
        "ne,nd->ed", context, whole_grad_mixer, preferred_element_type=jnp.float32
    )
    grad_items = grad_context.reshape(seq_count, blocks_count, BLK, head_local, HD).transpose(
        0, 3, 1, 2, 4
    )
    grad_items = grad_items.reshape(seq_count * head_local, blocks_count, BLK, HD)
    grad_stack = lax.map(run_backward, (items, chosen_all, grad_items, log_middle, log_edge))
    grad_projected = grad_stack.reshape(seq_count, head_local, 3, blocks_count, BLK, HD).transpose(
        2, 0, 3, 4, 1, 5
    )
    grad_projected = grad_projected.reshape(3, group_rows, head_local * HD)
    grad_bias_pair = jnp.stack(
        [
            jnp.sum(grad_projected[0], axis=0, dtype=jnp.float32),
            jnp.sum(grad_projected[2], axis=0, dtype=jnp.float32),
        ]
    ).reshape(2, head_local, HD)
    grad_qkv_weight = jnp.einsum(
        "nd,kne->kde", whole_in, grad_projected, preferred_element_type=jnp.float32
    )
    piece = grad_projected
    grad_tokens = grad_mixed + lax.psum_scatter(
        jnp.einsum("kne,kde->nd", piece, qkv_weight, preferred_element_type=jnp.float32).astype(
            jnp.bfloat16
        ),
        "tensor",
        scatter_dimension=0,
        tiled=True,
    ).astype(jnp.float32)
    grads = (
        lax.psum_scatter(grad_qkv_weight, "dp", scatter_dimension=1, tiled=True),
        lax.psum_scatter(grad_bias_pair, "dp", scatter_dimension=2, tiled=True),
        lax.psum_scatter(grad_out_weight, "dp", scatter_dimension=1, tiled=True),
        lax.psum_scatter(grad_in_weight, "dp", scatter_dimension=0, tiled=True),
        lax.psum_scatter(grad_in_bias, "dp", scatter_dimension=1, tiled=True),
        lax.psum_scatter(grad_back_weight, "dp", scatter_dimension=1, tiled=True),
    )
    gain_terms = jnp.stack([grad_gain_one, grad_gain_two])
    bias_terms = jnp.stack(
        [jnp.sum(grad_mixed, axis=0), grad_shift_one, jnp.sum(grad_second, axis=0), grad_shift_two]
    )
    vectors = (
        lax.psum_scatter(gain_terms, ("dp", "tensor"), scatter_dimension=1, tiled=True),
        lax.psum_scatter(bias_terms, ("dp", "tensor"), scatter_dimension=1, tiled=True),
    )
    return (
        loss,
        encoded,
        grad_tokens,
        grads[0],
        grads[1],
        grads[2],
        grads[3],
        grads[4],
        grads[5],
        vectors[0],
        vectors[1],
    )


def solution(mesh):
    in_specs = (
        P(("dp", "tensor"), None),
        P(("dp", "tensor"), None),
        P(("dp", "tensor")),
        P(),
        P(None, "dp", "tensor"),
        P(None, "tensor", "dp"),
        P("tensor", "dp"),
        P("dp", "tensor"),
        P("tensor", "dp"),
        P("tensor", "dp"),
        P(None, "dp"),
        P(None, "dp"),
    )
    out_specs = (
        P(),
        P(("dp", "tensor"), None),
        P(("dp", "tensor"), None),
        P(None, "dp", "tensor"),
        P(None, "tensor", "dp"),
        P("tensor", "dp"),
        P("dp", "tensor"),
        P("tensor", "dp"),
        P("tensor", "dp"),
        P(None, ("dp", "tensor")),
        P(None, ("dp", "tensor")),
    )
    return jax.shard_map(
        per_device, mesh=mesh, in_specs=in_specs, out_specs=out_specs, check_vma=False
    )
```

profile of v0, /device:TPU:0, one launch (start us, length us, event | category | flops | bytes accessed | tf_op | source)
XLA Modules:
  0.0 1814.6 jit_solution(15611825318617754182)
XLA Ops:
  10.3 32.2 %all_gather.47 = bf16[2,3,64]{1,0,2:T(2,128)(2,1)S(1)} all-gather(bf16[2,3,8]{1,0,2:T(2,128)(2,1)S(1)} %copy.288), channel_id=1, replica_groups=mesh['dp'=8,'tensor'=4] {'dp'}, dimensions={2}, use_global_device_ids=true | all-gather | bytes 864 | tf_op jit(solution)/shard_map/all_gather | solution.py:32
  44.8 31.3 %all_gather.48 = bf16[192,768]{0,1:T(8,128)(2,1)S(1)} all-gather(bf16[192,96]{0,1:T(8,128)(2,1)S(1)} %copy.293), channel_id=1, replica_groups=mesh['dp'=8,'tensor'=4] {'dp'}, dimensions={1}, use_global_device_ids=true | all-gather | bytes 331776 | tf_op jit(solution)/shard_map/all_gather | solution.py:33
  76.1 42.3 %all_gather.45 = bf16[3,768,192]{2,0,1:T(4,128)(2,1)S(1)} all-gather(bf16[3,96,192]{2,0,1:T(4,128)(2,1)S(1)} %copy.286), channel_id=1, replica_groups=mesh['dp'=8,'tensor'=4] {'dp'}, dimensions={1}, use_global_device_ids=true | all-gather | bytes 995328 | tf_op jit(solution)/shard_map/all_gather | solution.py:31
  130.0 13.8 reshape.654
  143.8 17.0 copy.291
  161.6 175.6 %while.28 = (s32[]{:T(128)}, bf16[6,32,64,64]{3,2,1,0:T(8,128)(2,1)}, f32[6,30,64]{2,1,0:T(8,128)S(1)}, f32[6,128]{1,0:T(8,128)S(1)}, bf16[6,3,32,64,64]{4,2,3,1...) while((s32[]{:T(128)}, ...), condition=%wide.region_5.6_spmd, body=%wide.region_0.5_spmd.sunk | while | flops 380113600 | bytes 35916652 | solution.py:239
  353.1 37.5 %psum.15 = f32[]{:T(128)} all-reduce(f32[]{:T(128)} %convert_reduce_fusion.2), channel_id=1, replica_groups=mesh['dp'=8,'tensor'=4] {'dp','tensor'}, use_global_device_ids=true, to_apply=%region_14.15 | all-reduce | flops 1 | bytes 8 | tf_op jit(solution)/shard_map/psum | solution.py:266
  390.6 20.0 %all-gather.1 = bf16[8,96,2]{1,2,0:T(2,128)(2,1)S(1)} all-gather(bf16[1,96,2]{1,2,0:T(2,128)(2,1)S(1)} %bitcast.468), channel_id=1, replica_groups=mesh['dp'=8,'tensor'=4] {'dp'}, dimensions={0}, use_global_device_ids=true | all-gather | bytes 3456 | tf_op jit(solution)/shard_map/all_gather | solution.py:37
  410.7 16.3 all-gather
  427.1 26.0 %all_gather.53 = bf16[12,64]{0,1:T(8,128)(2,1)S(1)} all-gather(bf16[12,8]{0,1:T(8,128)(2,1)S(1)} %copy-done.28), channel_id=1, replica_groups=mesh['dp'=8,'tensor'=4] {'dp'}, dimensions={1}, use_global_device_ids=true | all-gather | bytes 1728 | tf_op jit(solution)/shard_map/all_gather | solution.py:35
  473.4 13.5 all-gather.18.cloned.1.call-done
  507.9 20.5 %fusion.135 = (bf16[3072]{0:T(1024)(128)(2,1)}, bf16[1024,3072]{1,0:T(8,128)(2,1)}) fusion(bf16[3072,768]{0,1:T(8,128)(2,1)S(1)} %bitcast.472, f32[1024,768]{1,0:T(8,128)S(1)} %get-tuple-element.307, f32[1024]{0:T(1024)S(1)} %negate_multiply_fusion.1, f32[1024,3072]{1,0:T(8,128)} %fusion.126, f32[3072]{0:T(1024)S(1)} %reshape.666), kind=kOutput, calls=%fused_computation.289 | convolution fusion | flops 4915196928 | bytes 26761216 | tf_op jit(solution)/shard_map/nd,fd->nf/dot_general | solution.py:276
  566.0 22.7 %all-gather.20.cloned.1.call-done = bf16[4096,768]{1,0:T(8,128)(2,1)} async-done(((bf16[1024,768]{1,0:T(8,128)(2,1)}), bf16[4096,768]{1,0:T(8,128)(2,1)}) %all-gather.20.cloned.1.call-update) | async-done | bytes 6291472 | tf_op jit(solution)/shard_map/all_gather | solution.py:298
  610.3 881.7 %while.29 = (s32[]{:T(128)}, bf16[6,3,32,64,64]{4,3,2,1,0:T(8,128)(2,1)}, bf16[6,3,32,64,64]{4,2,3,1,0:T(8,128)(2,1)}, f32[6,128]{1,0:T(8,128)S(1)}, bf16[6,32,6...) while((s32[]{:T(128)}, ...), condition=%wide.region_26.27_spmd, body=%wide.region_19.26_spmd.sunk | while | flops 1145694464 | bytes 190884928 | solution.py:309
  686.3 16.3 slice_reduce_fusion.12
  729.1 16.4 slice_reduce_fusion.13
  828.5 16.3 slice_reduce_fusion.12
  871.2 16.4 slice_reduce_fusion.13
  970.6 16.3 slice_reduce_fusion.12
  1013.3 16.4 slice_reduce_fusion.13
  1112.6 16.3 slice_reduce_fusion.12
  1155.3 16.4 slice_reduce_fusion.13
  1254.7 16.3 slice_reduce_fusion.12
  1297.4 16.4 slice_reduce_fusion.13
  1396.7 16.3 slice_reduce_fusion.12
  1439.4 16.4 slice_reduce_fusion.13
  1492.0 13.5 copy.298
  1568.7 37.2 %all-reduce.13 = (f32[2,3,64]{2,1,0:T(4,128)S(1)}, f32[12,64]{1,0:T(8,128)S(1)}) all-reduce(f32[2,3,64]{2,1,0:T(4,128)S(1)} %pad_maximum_fusion.13, f32[12,64]{1,0:T(8,128)S(1)} %dynamic-slice_convert_fusion.2), channel_id=5, replica_groups=mesh['dp'=8,'tensor'=4] {'dp'}, use_global_device_ids=true, to_apply=%region_31.32.clone | all-reduce | flops 1152 | bytes 9216
  1610.9 50.1 %reduce-scatter.23.cloned.1.call-done = bf16[1024,768]{1,0:T(8,128)(2,1)} async-done(((bf16[4096,768]{1,0:T(8,128)(2,1)}), bf16[1024,768]{1,0:T(8,128)(2,1)}) %reduce-scatter.23.cloned.1.call-update) | async-done | bytes 1572880 | tf_op jit(solution)/shard_map/reduce_scatter | solution.py:324
  1665.5 40.4 %all-reduce.12 = (f32[]{:T(128)}, f32[2,768]{1,0:T(2,128)S(1)}, f32[4,768]{1,0:T(4,128)S(1)}) all-reduce(f32[]{:T(128)} %get-tuple-element.263, f32[2,768]{1,0:T(2,128)S(1)} %pad_maximum_fusion.11, f32[4,768]{1,0:T(4,128)S(1)} %pad_maximum_fusion.10), channel_id=1, replica_groups=mesh['dp'=8,'tensor'=4] {'dp','tensor'}, use_global_device_ids=true, to_apply=%region_12.13 | all-reduce | flops 4609 | bytes 36872 | tf_op jit(solution)/shard_map/psum | solution.py:266
  1707.9 26.9 %reduce-scatter.35.cloned.1.call-done = f32[96,768]{1,0:T(8,128)} async-done(((f32[768,768]{1,0:T(8,128)}), f32[96,768]{1,0:T(8,128)}) %reduce-scatter.35.cloned.1.call-update) | async-done | bytes 294928
  1734.8 72.0 %reduce-scatter.27.cloned.1.call-done = f32[96,768]{1,0:T(8,128)} async-done(((f32[768,768]{1,0:T(8,128)}), f32[96,768]{1,0:T(8,128)}) %reduce-scatter.27.cloned.1.call-update) | async-done | bytes 294928 | tf_op jit(solution)/shard_map/reduce_scatter | solution.py:336
  (870 shorter events, 1033.9 us)
Async XLA Ops:
  7.2 111.4 %copy-start = (s32[12,32,3,32]{3,1,2,0:T(8,128)S(1)}, s32[12,32,3,32]{3,1,2,0:T(8,128)}, u32[]{:S(2)}) copy-start(s32[12,32,3,32]{3,1,2,0:T(8,128)} %param.19) | copy-start | bytes 442372
  7.2 111.4 %all-gather.10.cloned.1.call-start = ((), (), s32[]{:S(2)}) async-start(), calls=%async_computation.8 | async-start | bytes 7864320 | tf_op jit(solution)/shard_map/all_gather | solution.py:229
  7.9 343.5 %all-gather.12.cloned.1.call-start = ((), (), s32[]{:S(2)}) async-start(), calls=%async_computation.10 | async-start | bytes 1327104 | tf_op jit(solution)/shard_map/all_gather | solution.py:34
  8.7 343.3 %all-gather.16.cloned.1.call-start = ((), (), s32[]{:S(2)}) async-start(), calls=%async_computation.12 | async-start | bytes 1327104 | tf_op jit(solution)/shard_map/all_gather | solution.py:36
  9.4 449.8 %reduce-scatter.21.cloned.1.call-start = ((), (), s32[]{:S(2)}) async-start(), calls=%async_computation.9 | async-start | bytes 7864320 | tf_op jit(solution)/shard_map/reduce_scatter | solution.py:245
  351.3 39.3 %copy-start.30 = (bf16[2,96]{1,0:T(2,128)(2,1)S(1)}, bf16[2,96]{1,0:T(2,128)(2,1)}, u32[]{:S(2)}) copy-start(bf16[2,96]{1,0:T(2,128)(2,1)} %param.26) | copy-start | bytes 1156
  351.3 59.5 %copy-start.29 = (bf16[4,96]{1,0:T(4,128)(2,1)S(1)}, bf16[4,96]{1,0:T(4,128)(2,1)}, u32[]{:S(2)}) copy-start(bf16[4,96]{1,0:T(4,128)(2,1)} %param.27) | copy-start | bytes 2308
  351.3 75.8 %copy-start.28 = (bf16[12,8]{0,1:T(8,128)(2,1)S(1)}, bf16[12,8]{0,1:T(8,128)(2,1)}, u32[]{:S(2)}) copy-start(bf16[12,8]{0,1:T(8,128)(2,1)} %param.24) | copy-start | bytes 580
  351.3 107.9 %copy-start.9 = (bf16[1024,768]{1,0:T(8,128)(2,1)S(1)}, bf16[1024,768]{1,0:T(8,128)(2,1)}, u32[]{:S(2)}) copy-start(bf16[1024,768]{1,0:T(8,128)(2,1)} %param.16) | copy-start | bytes 4718596
  351.3 111.0 %all-gather.14.cloned.1.call-start = ((), (), s32[]{:S(2)}) async-start(), calls=%async_computation.11 | async-start | bytes 5898240 | tf_op jit(solution)/shard_map/all_gather | solution.py:44
  351.9 135.0 %all-gather.18.cloned.1.call-start = ((), (), s32[]{:S(2)}) async-start(), calls=%async_computation.13 | async-start | bytes 5898240 | tf_op jit(solution)/shard_map/all_gather | solution.py:46
  352.5 236.3 %all-gather.20.cloned.1.call-start = ((), (), s32[]{:S(2)}) async-start(), calls=%async_computation.14 | async-start | bytes 7864320 | tf_op jit(solution)/shard_map/all_gather | solution.py:298
  506.2 22.3 %slice-start = ((s8[4718592]{0:T(1024)(128)(4,1)}), s8[524288]{0:T(1024)(128)(4,1)S(1)}, s32[]{:S(2)}) async-start(s8[4718592]{0:T(1024)(128)(4,1)} %bitcast.469), calls=%async_computation.22 | async-start | bytes 1048576
  507.8 20.6 %copy-start.12 = (f32[1024,768]{1,0:T(8,128)}, f32[1024,768]{1,0:T(8,128)S(1)}, u32[]{:S(2)}) copy-start(f32[1024,768]{1,0:T(8,128)S(1)} %get-tuple-element.307) | copy-start | bytes 9437188
  507.9 34.4 %copy-start.22 = (f32[1024]{0:T(1024)}, f32[1024]{0:T(1024)S(1)}, u32[]{:S(2)}) copy-start(f32[1024]{0:T(1024)S(1)} %negate_multiply_fusion.1) | copy-start | bytes 12292
  507.9 20.6 %copy-start.11 = (bf16[1024,768]{1,0:T(8,128)(2,1)S(1)}, bf16[1024,768]{1,0:T(8,128)(2,1)}, u32[]{:S(2)}) copy-start(bf16[1024,768]{1,0:T(8,128)(2,1)} %reduce-scatter.21.cloned.1.call-done) | copy-start | bytes 4718596
  507.9 20.6 %slice-start.1 = ((s8[4718592]{0:T(1024)(128)(4,1)}), s8[4194304]{0:T(1024)(128)(4,1)S(1)}, s32[]{:S(2)}) async-start(s8[4718592]{0:T(1024)(128)(4,1)} %bitcast.469), calls=%async_computation.23 | async-start | bytes 8388608
  542.2 1001.3 %reduce-scatter.29.cloned.1.call-start = ((), (), s32[]{:S(2)}) async-start(), calls=%async_computation.18 | async-start | bytes 5898240 | tf_op jit(solution)/shard_map/reduce_scatter | solution.py:290
  555.6 990.8 %reduce-scatter.25.cloned.1.call-start = ((), (), s32[]{:S(2)}) async-start(), calls=%async_computation.16 | async-start | bytes 5898240 | tf_op jit(solution)/shard_map/reduce_scatter | solution.py:284
  566.0 1041.4 %reduce-scatter.33.cloned.1.call-start = ((), (), s32[]{:S(2)}) async-start(), calls=%async_computation.20 | async-start | bytes 884736
  610.3 998.8 %reduce-scatter.31.cloned.1.call-start = ((), (), s32[]{:S(2)}) async-start(), calls=%async_computation.19 | async-start | bytes 2211840
  729.1 16.4 copy-start.3
  1013.3 16.4 copy-start.3
  1297.4 16.4 copy-start.3
  1533.8 127.2 %reduce-scatter.23.cloned.1.call-start = ((), (), s32[]{:S(2)}) async-start(), calls=%async_computation.15 | async-start | bytes 7864320 | tf_op jit(solution)/shard_map/reduce_scatter | solution.py:324
  1543.5 191.3 %reduce-scatter.35.cloned.1.call-start = ((), (), s32[]{:S(2)}) async-start(), calls=%async_computation.21 | async-start | bytes 2654208
  1546.3 17.7 copy-start.20
  1546.3 17.7 copy-start.26
  1546.3 260.4 %reduce-scatter.27.cloned.1.call-start = ((), (), s32[]{:S(2)}) async-start(), calls=%async_computation.17 | async-start | bytes 2654208 | tf_op jit(solution)/shard_map/reduce_scatter | solution.py:336
  1560.5 3.6 collective-permute-start
  1564.3 96.7 %copy-start.19 = (f32[1024]{0:T(1024)S(1)}, f32[1024]{0:T(1024)}, u32[]{:S(2)}) copy-start(f32[1024]{0:T(1024)} %copy-done.18) | copy-start | bytes 12292
  1610.2 196.6 %copy-start.1 = (s32[12,32,3,32]{3,1,2,0:T(8,128)S(1)}, s32[12,32,3,32]{3,1,2,0:T(8,128)}, u32[]{:S(2)}) copy-start(s32[12,32,3,32]{3,1,2,0:T(8,128)} %param.19) | copy-start | bytes 442372
  (50 other events, 378.5 us)
Sparse Core Ops, SparseCore 0:
  9.6 49.0 all-gather.9
  60.9 50.5 all-gather.11
  113.6 40.8 all-gather.15
  351.4 57.4 reduce-scatter.20
  410.4 37.4 all-gather.13
  449.4 37.4 all-gather.17
  542.3 46.3 all-gather.19
  591.4 47.8 reduce-scatter.28
  641.9 47.8 reduce-scatter.24
  693.2 62.4 reduce-scatter.32
  1533.9 67.1 reduce-scatter.30
  1603.6 57.3 reduce-scatter.22
  1665.1 69.6 reduce-scatter.34
  1738.7 67.9 reduce-scatter.26
where the time goes:
time: 1830 us; the launch traced here: 1810 us
  local copies, waits for them, and re-layouts  596 us (33%)
  matrix products  389 us (21%)
  blocking collectives  296 us (16%)
  other arithmetic  291 us (16%)
  waiting for transfers between devices  188 us (10%)
  loops' own time  32 us (2%)
  between operations  19.2 us (1%)
    while x216, local copies, waits for them, and re-layouts  240 us
    reduce_sum x12, other arithmetic, spread_slots(): jnp.sum(parts_grad[:, 3], axis=0)[None]  196 us
    reshape x12, local copies, waits for them, and re-layouts, spread_slots(): parts_grad = slot_grads.reshape(middle, -1, BLK, slot_grads.shape[-1])  80 us
    psum x2, blocking collectives, per_device(): lax.psum((jnp.sum(mask_rows[:, None] * error * error), jnp.sum(mask_rows)...  77.9 us
    reduce_scatter x1, waiting for transfers between devices, per_device(): lax.psum_scatter(grad_in_weight, 'dp', scatter_dimension=0, tiled=True)  72 us
    reduce_scatter x1, waiting for transfers between devices, per_device(): lax.psum_scatter(jnp.einsum('kne,kde->nd', piece, qkv_weight, preferred_e...  50.1 us
    dot_general x12, matrix products, middle_scores(): jnp.einsum('mqd,mkd->mqk', mid_queries, key_slots, preferred_element_type...  47.5 us
    unnamed x2, blocking collectives  45.1 us
  transfers between devices with their start and end apart: 15, of which 5 were waited for; matrix products, arithmetic and copies ran while one was open for 67% of the time, Pallas kernels for 0%

commit v1 on v0

--- a/solution.py
+++ b/solution.py
@@ -12,6 +12,28 @@
 exact_precision = lax.Precision.HIGHEST
 
 
+def laid_out(parts, dim):
+    parts = jnp.moveaxis(parts, 0, dim)
+    shape = parts.shape
+    return parts.reshape(*shape[:dim], shape[dim] * shape[dim + 1], *shape[dim + 2 :])
+
+
+def grow_blocks(x, axis):
+    size = lax.axis_size(axis)
+    pieces = x[None]
+    for level in range(size.bit_length() - 1):
+        bit = 1 << level
+        other = lax.ppermute(pieces, axis, [(i, i ^ bit) for i in range(size)])
+        both = jnp.stack([pieces, other])
+        upper = lax.axis_index(axis) >> level & 1
+        pieces = jnp.where(upper == 0, both, both[::-1]).reshape(-1, *x.shape)
+    return pieces
+
+
+def collect(x, axis, dim):
+    return laid_out(grow_blocks(x, axis), dim)
+
+
 def layer_norm(values, gain, shift):
     centred = values - jnp.mean(values, axis=-1, keepdims=True)
     variance = jnp.mean(centred * centred, axis=-1, keepdims=True)
@@ -28,7 +50,7 @@
 
 def fetch_weights(w_qkv, b_qv, w_out, w_in, b_in, w_back, ln_gains, row_biases):
     return (
-        lax.all_gather(w_qkv, "dp", axis=1, tiled=True),
+        collect(w_qkv, "dp", 1),
         lax.all_gather(b_qv, "dp", axis=2, tiled=True),
         lax.all_gather(w_out, "dp", axis=1, tiled=True),
         lax.all_gather(w_in, "dp", axis=0, tiled=True),

time: 1830 us -> 1820 us (level)
  blocking collectives: 296 us -> 265 us
    all_gather x1 -> x0, blocking collectives: 42.3 us -> none  [fetch_weights(): lax.all_gather(w_qkv, 'dp', axis=1, tiled=True)]
  transfers between devices with their start and end apart: 15 -> 18, of which waited for: 5 -> 6; matrix products, arithmetic and copies ran while one was open for 67% -> 68% of each run, Pallas kernels for 0% -> 0%
where the time goes in v1:
time: 1820 us; the launch traced here: 1800 us
  local copies, waits for them, and re-layouts  603 us (33%)
  matrix products  386 us (21%)
  other arithmetic  297 us (16%)
  blocking collectives  265 us (15%)
  waiting for transfers between devices  195 us (11%)
  loops' own time  31.9 us (2%)
  between operations  19.3 us (1%)
    while x216, local copies, waits for them, and re-layouts  241 us
    reduce_sum x12, other arithmetic, spread_slots(): jnp.sum(parts_grad[:, 3], axis=0)[None]  197 us
    reshape x12, local copies, waits for them, and re-layouts, spread_slots(): parts_grad = slot_grads.reshape(middle, -1, BLK, slot_grads.shape[-1])  80 us
    psum x2, blocking collectives, per_device(): lax.psum((jnp.sum(mask_rows[:, None] * error * error), jnp.sum(mask_rows)...  78.2 us
    reduce_scatter x1, waiting for transfers between devices, per_device(): lax.psum_scatter(grad_in_weight, 'dp', scatter_dimension=0, tiled=True)  72 us
    reduce_scatter x1, waiting for transfers between devices, per_device(): lax.psum_scatter(jnp.einsum('kne,kde->nd', piece, qkv_weight, preferred_e...  50.6 us
    dot_general x12, matrix products, middle_scores(): jnp.einsum('mqd,mkd->mqk', mid_queries, key_slots, preferred_element_type...  47.5 us
    unnamed x2, blocking collectives  44.7 us
  transfers between devices with their start and end apart: 18, of which 6 were waited for; matrix products, arithmetic and copies ran while one was open for 68% of the time, Pallas kernels for 0%

profile of v1, /device:TPU:0, one launch (start us, length us, event | category | flops | bytes accessed | tf_op | source)
XLA Modules:
  0.0 1801.9 jit_solution(16670056493569481237)
XLA Ops:
  12.6 30.8 %all_gather.42 = bf16[2,3,64]{1,0,2:T(2,128)(2,1)S(1)} all-gather(bf16[2,3,8]{1,0,2:T(2,128)(2,1)S(1)} %copy.280), channel_id=1, replica_groups=mesh['dp'=8,'tensor'=4] {'dp'}, dimensions={2}, use_global_device_ids=true | all-gather | bytes 864 | tf_op jit(solution)/shard_map/all_gather | solution.py:54
  54.1 43.6 %all_gather.43 = bf16[192,768]{0,1:T(8,128)(2,1)S(1)} all-gather(bf16[192,96]{0,1:T(8,128)(2,1)S(1)} %copy.285), channel_id=1, replica_groups=mesh['dp'=8,'tensor'=4] {'dp'}, dimensions={1}, use_global_device_ids=true | all-gather | bytes 331776 | tf_op jit(solution)/shard_map/all_gather | solution.py:55
  109.3 13.8 reshape.674
  123.1 16.9 copy.283
  140.8 179.1 %while.28 = (s32[]{:T(128)}, bf16[6,32,64,64]{3,2,1,0:T(8,128)(2,1)}, f32[6,30,64]{2,1,0:T(8,128)}, f32[6,128]{1,0:T(8,128)S(1)}, bf16[6,3,32,64,64]{4,2,3,1,0:T...) while((s32[]{:T(128)}, ...), condition=%wide.region_5.6_spmd, body=%wide.region_0.5_spmd.sunk | while | flops 380113600 | bytes 35890540 | solution.py:261
  335.8 37.6 %psum.15 = f32[]{:T(128)} all-reduce(f32[]{:T(128)} %convert_reduce_fusion.2), channel_id=1, replica_groups=mesh['dp'=8,'tensor'=4] {'dp','tensor'}, use_global_device_ids=true, to_apply=%region_14.15 | all-reduce | flops 1 | bytes 8 | tf_op jit(solution)/shard_map/psum | solution.py:288
  373.4 19.9 %all-gather.1 = bf16[8,96,2]{1,2,0:T(2,128)(2,1)S(1)} all-gather(bf16[1,96,2]{1,2,0:T(2,128)(2,1)S(1)} %bitcast.496), channel_id=1, replica_groups=mesh['dp'=8,'tensor'=4] {'dp'}, dimensions={0}, use_global_device_ids=true | all-gather | bytes 3456 | tf_op jit(solution)/shard_map/all_gather | solution.py:59
  393.4 16.3 all-gather
  409.8 26.0 %all_gather.48 = bf16[12,64]{0,1:T(8,128)(2,1)S(1)} all-gather(bf16[12,8]{0,1:T(8,128)(2,1)S(1)} %copy-done.28), channel_id=1, replica_groups=mesh['dp'=8,'tensor'=4] {'dp'}, dimensions={1}, use_global_device_ids=true | all-gather | bytes 1728 | tf_op jit(solution)/shard_map/all_gather | solution.py:57
  468.7 13.1 fusion.134
  489.7 20.6 %fusion.135 = (bf16[3072]{0:T(1024)(128)(2,1)}, bf16[1024,3072]{1,0:T(8,128)(2,1)}) fusion(bf16[3072,768]{0,1:T(8,128)(2,1)S(1)} %bitcast.500, f32[1024,768]{1,0:T(8,128)S(1)} %get-tuple-element.307, f32[1024]{0:T(1024)S(1)} %negate_multiply_fusion.1, f32[1024,3072]{1,0:T(8,128)} %fusion.126, f32[3072]{0:T(1024)S(1)} %reshape.686), kind=kOutput, calls=%fused_computation.295 | convolution fusion | flops 4915196928 | bytes 26761216 | tf_op jit(solution)/shard_map/nd,fd->nf/dot_general | solution.py:298
  524.1 13.4 convolution_convert_fusion.6
  547.9 22.6 %all-gather.20.cloned.1.call-done = bf16[4096,768]{1,0:T(8,128)(2,1)} async-done(((bf16[1024,768]{1,0:T(8,128)(2,1)}), bf16[4096,768]{1,0:T(8,128)(2,1)}) %all-gather.20.cloned.1.call-update) | async-done | bytes 6291472 | tf_op jit(solution)/shard_map/all_gather | solution.py:320
  592.2 887.4 %while.29 = (s32[]{:T(128)}, bf16[6,3,32,64,64]{4,3,2,1,0:T(8,128)(2,1)}, bf16[6,3,32,64,64]{4,2,3,1,0:T(8,128)(2,1)}, f32[6,128]{1,0:T(8,128)S(1)}, bf16[6,32,6...) while((s32[]{:T(128)}, ...), condition=%wide.region_26.27_spmd, body=%wide.region_19.26_spmd.sunk | while | flops 1145694464 | bytes 190884928 | solution.py:331
  669.1 16.3 slice_reduce_fusion.12
  712.1 16.5 slice_reduce_fusion.13
  812.2 16.3 slice_reduce_fusion.12
  855.1 16.5 slice_reduce_fusion.13
  955.3 16.3 slice_reduce_fusion.12
  998.1 16.5 slice_reduce_fusion.13
  1098.2 16.3 slice_reduce_fusion.12
  1141.1 16.5 slice_reduce_fusion.13
  1241.3 16.3 slice_reduce_fusion.12
  1284.1 16.5 slice_reduce_fusion.13
  1384.3 16.3 slice_reduce_fusion.12
  1427.1 16.5 slice_reduce_fusion.13
  1479.6 13.6 copy.290
  1556.1 36.9 %all-reduce.13 = (f32[2,3,64]{2,1,0:T(4,128)S(1)}, f32[12,64]{1,0:T(8,128)S(1)}) all-reduce(f32[2,3,64]{2,1,0:T(4,128)S(1)} %pad_maximum_fusion.16, f32[12,64]{1,0:T(8,128)S(1)} %dynamic-slice_convert_fusion.2), channel_id=5, replica_groups=mesh['dp'=8,'tensor'=4] {'dp'}, use_global_device_ids=true, to_apply=%region_31.32.clone | all-reduce | flops 1152 | bytes 9216
  1598.0 50.6 %reduce-scatter.23.cloned.1.call-done = bf16[1024,768]{1,0:T(8,128)(2,1)} async-done(((bf16[4096,768]{1,0:T(8,128)(2,1)}), bf16[1024,768]{1,0:T(8,128)(2,1)}) %reduce-scatter.23.cloned.1.call-update) | async-done | bytes 1572880 | tf_op jit(solution)/shard_map/reduce_scatter | solution.py:346
  1653.1 40.6 %all-reduce.12 = (f32[]{:T(128)}, f32[2,768]{1,0:T(2,128)S(1)}, f32[4,768]{1,0:T(4,128)S(1)}) all-reduce(f32[]{:T(128)} %get-tuple-element.263, f32[2,768]{1,0:T(2,128)S(1)} %pad_maximum_fusion.14, f32[4,768]{1,0:T(4,128)S(1)} %pad_maximum_fusion.13), channel_id=1, replica_groups=mesh['dp'=8,'tensor'=4] {'dp','tensor'}, use_global_device_ids=true, to_apply=%region_12.13 | all-reduce | flops 4609 | bytes 36872 | tf_op jit(solution)/shard_map/psum | solution.py:288
  1695.6 26.4 %reduce-scatter.35.cloned.1.call-done = f32[96,768]{1,0:T(8,128)} async-done(((f32[768,768]{1,0:T(8,128)}), f32[96,768]{1,0:T(8,128)}) %reduce-scatter.35.cloned.1.call-update) | async-done | bytes 294928
  1722.0 72.0 %reduce-scatter.27.cloned.1.call-done = f32[96,768]{1,0:T(8,128)} async-done(((f32[768,768]{1,0:T(8,128)}), f32[96,768]{1,0:T(8,128)}) %reduce-scatter.27.cloned.1.call-update) | async-done | bytes 294928 | tf_op jit(solution)/shard_map/reduce_scatter | solution.py:358
  (882 shorter events, 1039.3 us)
Async XLA Ops:
  7.2 46.9 %copy-start = (s32[12,32,3,32]{3,1,2,0:T(8,128)S(1)}, s32[12,32,3,32]{3,1,2,0:T(8,128)}, u32[]{:S(2)}) copy-start(s32[12,32,3,32]{3,1,2,0:T(8,128)} %param.19) | copy-start | bytes 442372
  7.2 93.5 %all-gather.10.cloned.1.call-start = ((), (), s32[]{:S(2)}) async-start(), calls=%async_computation.8 | async-start | bytes 7864320 | tf_op jit(solution)/shard_map/all_gather | solution.py:251
  7.9 326.2 %all-gather.12.cloned.1.call-start = ((), (), s32[]{:S(2)}) async-start(), calls=%async_computation.10 | async-start | bytes 1327104 | tf_op jit(solution)/shard_map/all_gather | solution.py:56
  8.7 326.0 %all-gather.16.cloned.1.call-start = ((), (), s32[]{:S(2)}) async-start(), calls=%async_computation.12 | async-start | bytes 1327104 | tf_op jit(solution)/shard_map/all_gather | solution.py:58
  8.7 34.7 %collective-permute-start = (bf16[1,3,96,192]{3,2,1,0:T(8,128)(2,1)}, bf16[1,3,96,192]{3,2,1,0:T(8,128)(2,1)S(1)}, u32[]{:S(2)}, u32[]{:S(2)}) collective-permute-start(bf16[1,3,96,192]{3,2,1,0:T(8,128)(2,1)} %bitcast.485), channel_id=1, source_target_pairs={{0,4},{4,0},{8,12},{12,8},{16,20},{20,16},{24,28},{28,24},{1,5},{5... | collective-permute-start | bytes 331784 | tf_op jit(solution)/shard_map/ppermute | solution.py:26
  11.8 430.2 %reduce-scatter.21.cloned.1.call-start = ((), (), s32[]{:S(2)}) async-start(), calls=%async_computation.9 | async-start | bytes 7864320 | tf_op jit(solution)/shard_map/reduce_scatter | solution.py:267
  44.5 9.3 collective-permute-start.1
  54.0 43.7 %collective-permute-start.2 = (bf16[4,3,96,192]{3,2,1,0:T(8,128)(2,1)S(1)}, bf16[4,3,96,192]{3,2,1,0:T(8,128)(2,1)S(1)}, u32[]{:S(2)}, u32[]{:S(2)}) collective-permute-start(bf16[4,3,96,192]{3,2,1,0:T(8,128)(2,1)S(1)} %bitcast.479), channel_id=1, source_target_pairs={{0,16},{4,20},{8,24},{12,28},{16,0},{20,4},{24,8},{28,12},{1,17},{... | collective-permute-start | bytes 1327112 | tf_op jit(solution)/shard_map/ppermute | solution.py:26
  334.0 39.5 %copy-start.30 = (bf16[2,96]{1,0:T(2,128)(2,1)S(1)}, bf16[2,96]{1,0:T(2,128)(2,1)}, u32[]{:S(2)}) copy-start(bf16[2,96]{1,0:T(2,128)(2,1)} %param.26) | copy-start | bytes 1156
  334.0 59.5 %copy-start.29 = (bf16[4,96]{1,0:T(4,128)(2,1)S(1)}, bf16[4,96]{1,0:T(4,128)(2,1)}, u32[]{:S(2)}) copy-start(bf16[4,96]{1,0:T(4,128)(2,1)} %param.27) | copy-start | bytes 2308
  334.0 75.8 %copy-start.28 = (bf16[12,8]{0,1:T(8,128)(2,1)S(1)}, bf16[12,8]{0,1:T(8,128)(2,1)}, u32[]{:S(2)}) copy-start(bf16[12,8]{0,1:T(8,128)(2,1)} %param.24) | copy-start | bytes 580
  334.0 108.0 %copy-start.9 = (bf16[1024,768]{1,0:T(8,128)(2,1)S(1)}, bf16[1024,768]{1,0:T(8,128)(2,1)}, u32[]{:S(2)}) copy-start(bf16[1024,768]{1,0:T(8,128)(2,1)} %param.16) | copy-start | bytes 4718596
  334.0 111.0 %all-gather.14.cloned.1.call-start = ((), (), s32[]{:S(2)}) async-start(), calls=%async_computation.11 | async-start | bytes 5898240 | tf_op jit(solution)/shard_map/all_gather | solution.py:66
  334.6 134.1 %all-gather.18.cloned.1.call-start = ((), (), s32[]{:S(2)}) async-start(), calls=%async_computation.13 | async-start | bytes 5898240 | tf_op jit(solution)/shard_map/all_gather | solution.py:68
  335.2 235.4 %all-gather.20.cloned.1.call-start = ((), (), s32[]{:S(2)}) async-start(), calls=%async_computation.14 | async-start | bytes 7864320 | tf_op jit(solution)/shard_map/all_gather | solution.py:320
  487.9 22.4 %slice-start = ((s8[4718592]{0:T(1024)(128)(4,1)}), s8[524288]{0:T(1024)(128)(4,1)S(1)}, s32[]{:S(2)}) async-start(s8[4718592]{0:T(1024)(128)(4,1)} %bitcast.497), calls=%async_computation.22 | async-start | bytes 1048576
  489.6 20.7 %copy-start.12 = (f32[1024,768]{1,0:T(8,128)}, f32[1024,768]{1,0:T(8,128)S(1)}, u32[]{:S(2)}) copy-start(f32[1024,768]{1,0:T(8,128)S(1)} %get-tuple-element.307) | copy-start | bytes 9437188
  489.6 34.5 %copy-start.22 = (f32[1024]{0:T(1024)}, f32[1024]{0:T(1024)S(1)}, u32[]{:S(2)}) copy-start(f32[1024]{0:T(1024)S(1)} %negate_multiply_fusion.1) | copy-start | bytes 12292
  489.7 20.6 %copy-start.11 = (bf16[1024,768]{1,0:T(8,128)(2,1)S(1)}, bf16[1024,768]{1,0:T(8,128)(2,1)}, u32[]{:S(2)}) copy-start(bf16[1024,768]{1,0:T(8,128)(2,1)} %reduce-scatter.21.cloned.1.call-done) | copy-start | bytes 4718596
  489.7 20.6 %slice-start.1 = ((s8[4718592]{0:T(1024)(128)(4,1)}), s8[4194304]{0:T(1024)(128)(4,1)S(1)}, s32[]{:S(2)}) async-start(s8[4718592]{0:T(1024)(128)(4,1)} %bitcast.497), calls=%async_computation.23 | async-start | bytes 8388608
  524.0 1006.9 %reduce-scatter.29.cloned.1.call-start = ((), (), s32[]{:S(2)}) async-start(), calls=%async_computation.18 | async-start | bytes 5898240 | tf_op jit(solution)/shard_map/reduce_scatter | solution.py:312
  537.6 996.3 %reduce-scatter.25.cloned.1.call-start = ((), (), s32[]{:S(2)}) async-start(), calls=%async_computation.16 | async-start | bytes 5898240 | tf_op jit(solution)/shard_map/reduce_scatter | solution.py:306
  547.9 1046.5 %reduce-scatter.33.cloned.1.call-start = ((), (), s32[]{:S(2)}) async-start(), calls=%async_computation.20 | async-start | bytes 884736
  592.1 1003.9 %reduce-scatter.31.cloned.1.call-start = ((), (), s32[]{:S(2)}) async-start(), calls=%async_computation.19 | async-start | bytes 2211840
  1521.3 127.2 %reduce-scatter.23.cloned.1.call-start = ((), (), s32[]{:S(2)}) async-start(), calls=%async_computation.15 | async-start | bytes 7864320 | tf_op jit(solution)/shard_map/reduce_scatter | solution.py:346
  1530.9 191.1 %reduce-scatter.35.cloned.1.call-start = ((), (), s32[]{:S(2)}) async-start(), calls=%async_computation.21 | async-start | bytes 2654208
  1533.8 17.6 copy-start.20
  1533.8 17.7 copy-start.26
  1533.8 260.2 %reduce-scatter.27.cloned.1.call-start = ((), (), s32[]{:S(2)}) async-start(), calls=%async_computation.17 | async-start | bytes 2654208 | tf_op jit(solution)/shard_map/reduce_scatter | solution.py:358
  1547.9 3.6 collective-permute-start.3
  1551.7 96.9 %copy-start.19 = (f32[1024]{0:T(1024)S(1)}, f32[1024]{0:T(1024)}, u32[]{:S(2)}) copy-start(f32[1024]{0:T(1024)} %copy-done.18) | copy-start | bytes 12292
  1597.2 196.8 %copy-start.1 = (s32[12,32,3,32]{3,1,2,0:T(8,128)S(1)}, s32[12,32,3,32]{3,1,2,0:T(8,128)}, u32[]{:S(2)}) copy-start(s32[12,32,3,32]{3,1,2,0:T(8,128)} %param.19) | copy-start | bytes 442372
  (53 other events, 425.8 us)
Sparse Core Ops, SparseCore 0:
  9.6 49.0 all-gather.9
  60.9 43.0 all-gather.11
  106.2 40.3 all-gather.15
  334.1 56.5 reduce-scatter.20
  392.2 37.4 all-gather.13
  431.2 37.4 all-gather.17
  524.2 46.3 all-gather.19
  573.3 47.8 reduce-scatter.28
  623.7 47.8 reduce-scatter.24
  675.0 62.4 reduce-scatter.32
  1521.5 67.0 reduce-scatter.30
  1591.1 57.4 reduce-scatter.22
  1652.6 69.3 reduce-scatter.34
  1725.9 68.0 reduce-scatter.26
